TPU v7x, 32 devices: a whole 2x2x4 slice. The times are simulated.
32 devices in a mesh: row: 8 (over z, x), col: 4 (over y, core).
Axes of the slice: x: 2, y: 2, z: 4, core: 2. Of those that a mesh axis runs over, the one named last changes fastest.
Arguments:
- features: bfloat16 [8192, 256], P(('row', 'col')), may hold values from -6 to 6
- grad_out: bfloat16 [8192, 256], P(('row', 'col')), may hold values from -6 to 6
- degrees: int32 [8192], P(('row', 'col')), may hold values from 1 to 8236, as said below
- w_self: bfloat16 [256, 256], replicated, may hold values from -0.375 to 0.375
- w_neigh: bfloat16 [256, 256], replicated, may hold values from -0.375 to 0.375
- bias: float32 [256], replicated, may hold values from -4 to 4
- tile_slots: int32 [8, 4, 88], P('row', 'col'), may hold values from 0 to 127, as said below
- tile_count: int32 [8, 4], P('row', 'col'), may hold values from 22 to 88, as said below
- tile_masks: int32 [8, 4, 88, 16, 128], P('row', 'col'), may hold values from 0 to 255
Outputs:
- layer_out: bfloat16 [8192, 256], P(('row', 'col'))
- grad_in: bfloat16 [8192, 256], P(('row', 'col'))
- grad_w_self: float32 [256, 256], replicated
- grad_w_neigh: float32 [256, 256], replicated
Inputs may be any that keep to these rules, and one draw needn't show every extreme that they name: `tile_slots`: on each device the 88 slot numbers are distinct and rise; slot s names block row s % 8 of the device's row group and block column s // 8 of its panel. Only a device's first tile_count tiles are live; the others are ignored. Some device holds 88 live tiles. `degrees`: each node's degree is at least the number of ones in its row of A, and at least 1; some node has the largest degree.
All inputs are finite; a program needn't handle non-finite values.
Results may differ from a plain program's by a relative error of at most 0.014.
Values may be sent and summed in bfloat16 or wider, within the bound.
No kernel may reach another device: no remote copies, remote signals or barrier semaphores. Data moves between devices by JAX's collectives and lax.ppermute only.
A program may use at most 64 MiB of HBM per device.

v0:
```python
import math
import jax
import jax.numpy as jnp
from jax import lax
from jax.sharding import PartitionSpec as P

group_tiles = 8


def unpack_tiles(mask_words):
    shifts = jnp.arange(8, dtype=jnp.int32)
    bit_values = jnp.bitwise_and(
        jnp.right_shift(mask_words[:, :, None, :], shifts[None, None, :, None]), 1
    )
    return bit_values.reshape(mask_words.shape[0], mask_words.shape[1] * 8, mask_words.shape[2])


def tile_range(slot_ids, live_count, block_rows, low_column, high_column, tile_width):
    column_block = slot_ids // block_rows
    positions = jnp.arange(slot_ids.shape[0], dtype=jnp.int32)
    is_live = positions < live_count
    first_tile = jnp.sum(
        jnp.logical_and(is_live, (column_block + 1) * tile_width <= low_column).astype(jnp.int32)
    )
    last_tile = jnp.sum(
        jnp.logical_and(is_live, column_block * tile_width < high_column).astype(jnp.int32)
    )
    return (first_tile, last_tile)


def aggregate_piece(totals, panel_piece, first_row, slot_ids, live_count, mask_words):
    tile_width = mask_words.shape[2]
    block_rows = totals.shape[0] // tile_width
    piece_rows = panel_piece.shape[0]
    feature_width = panel_piece.shape[1]
    first_tile, last_tile = tile_range(
        slot_ids, live_count, block_rows, first_row, first_row + piece_rows, tile_width
    )
    margin = jnp.zeros((tile_width, feature_width), panel_piece.dtype)
    padded = jnp.concatenate([margin, panel_piece, margin], axis=0)
    group_count = (last_tile - first_tile + group_tiles - 1) // group_tiles
    within = jnp.arange(group_tiles, dtype=jnp.int32)
    tile_columns = jnp.arange(tile_width, dtype=jnp.int32)

    def aggregate_one_group(group_index, running):
        chosen = first_tile + group_index * group_tiles + within
        in_range = chosen < last_tile
        chosen = jnp.minimum(chosen, slot_ids.shape[0] - 1)
        chosen_slots = slot_ids[chosen]
        row_block = chosen_slots % block_rows
        column_block = chosen_slots // block_rows
        columns = column_block[:, None] * tile_width + tile_columns[None, :]
        keep_mask = in_range[:, None] & (columns >= first_row) & (columns < first_row + piece_rows)
        tile_bits = unpack_tiles(mask_words[chosen]) * keep_mask[:, :, None].astype(jnp.int32)
        offsets = column_block * tile_width - first_row + tile_width
        blocks = jax.vmap(lambda offset: lax.dynamic_slice_in_dim(padded, offset, tile_width, 0))(
            offsets
        )
        products = jnp.einsum(
            "gji,gjf->gif",
            tile_bits.astype(jnp.bfloat16),
            blocks,
            preferred_element_type=jnp.float32,
        )
        shaped = running.reshape(block_rows, tile_width, feature_width)
        return shaped.at[row_block].add(products).reshape(running.shape)

    return lax.fori_loop(0, group_count, aggregate_one_group, totals)


def spread_rows(first_row, row_count, slot_ids, live_count, mask_words, upward_rows):
    tile_width = mask_words.shape[2]
    block_rows = upward_rows.shape[0] // tile_width
    feature_width = upward_rows.shape[1]
    first_tile, last_tile = tile_range(
        slot_ids, live_count, block_rows, first_row, first_row + row_count, tile_width
    )
    first_block = first_row // tile_width
    upward_blocks = upward_rows.reshape(block_rows, tile_width, feature_width)
    group_count = (last_tile - first_tile + group_tiles - 1) // group_tiles
    within = jnp.arange(group_tiles, dtype=jnp.int32)

    def spread_one_group(group_index, running):
        chosen = first_tile + group_index * group_tiles + within
        in_range = chosen < last_tile
        chosen = jnp.minimum(chosen, slot_ids.shape[0] - 1)
        chosen_slots = slot_ids[chosen]
        row_block = chosen_slots % block_rows
        column_block = chosen_slots // block_rows
        tile_bits = unpack_tiles(mask_words[chosen]) * in_range[:, None, None].astype(jnp.int32)
        sources = upward_blocks[row_block]
        products = jnp.einsum(
            "gji,gif->gjf",
            tile_bits.astype(jnp.bfloat16),
            sources,
            preferred_element_type=jnp.float32,
        )
        return running.at[column_block - first_block].add(products)

    initial = jnp.zeros((row_count // tile_width, tile_width, feature_width), jnp.float32)
    partial_value = lax.fori_loop(0, group_count, spread_one_group, initial)
    return partial_value.reshape(row_count, feature_width)


def shards(features, grad_out, degrees, w_self, w_neigh, bias, tile_slots, tile_count, tile_masks):
    slot_ids = tile_slots[0, 0]
    live_count = tile_count[0, 0]
    mask_words = tile_masks[0, 0]
    node_rows, feature_width = features.shape
    group_size = node_rows * lax.axis_size("col")
    initial = jnp.zeros((group_size, feature_width), jnp.float32)
    panel = lax.all_gather(features, "row", axis=0, tiled=True)
    partial_value = aggregate_piece(initial, panel, 0, slot_ids, live_count, mask_words)
    summed = lax.psum_scatter(
        partial_value.astype(jnp.bfloat16), "col", scatter_dimension=0, tiled=True
    ).astype(jnp.float32)
    scale_degree = degrees.astype(jnp.float32)[:, None]
    mean_rows = (summed / scale_degree).astype(jnp.bfloat16)
    preact = jnp.dot(features, w_self, preferred_element_type=jnp.float32)
    preact = preact + jnp.dot(mean_rows, w_neigh, preferred_element_type=jnp.float32) + bias
    sigmoid_values = jax.nn.sigmoid(preact)
    layer_out = (preact * sigmoid_values).astype(jnp.bfloat16)
    grad_preact = (
        grad_out.astype(jnp.float32) * sigmoid_values * (1.0 + preact * (1.0 - sigmoid_values))
    ).astype(jnp.bfloat16)
    contract_rows = (((0,), (0,)), ((), ()))
    contract_cols = (((1,), (1,)), ((), ()))
    grad_self = lax.dot_general(
        features, grad_preact, contract_rows, preferred_element_type=jnp.float32
    )
    grad_neigh = lax.dot_general(
        mean_rows, grad_preact, contract_rows, preferred_element_type=jnp.float32
    )
    grad_self, grad_neigh = lax.psum((grad_self, grad_neigh), ("row", "col"))
    grad_scale = 1.0 / math.sqrt(node_rows * lax.axis_size("row") * lax.axis_size("col"))
    upward = lax.dot_general(
        grad_preact, w_neigh, contract_cols, preferred_element_type=jnp.float32
    )
    upward = (upward / scale_degree).astype(jnp.bfloat16)
    upward_rows = lax.all_gather(upward, "col", axis=0, tiled=True)
    panel_size = node_rows * lax.axis_size("row")
    neighbor_grad = lax.psum_scatter(
        spread_rows(0, panel_size, slot_ids, live_count, mask_words, upward_rows).astype(
            jnp.bfloat16
        ),
        "row",
        scatter_dimension=0,
        tiled=True,
    ).astype(jnp.float32)
    self_grad = lax.dot_general(
        grad_preact, w_self, contract_cols, preferred_element_type=jnp.float32
    )
    grad_in = (self_grad + neighbor_grad).astype(jnp.bfloat16)
    return (layer_out, grad_in, grad_self * grad_scale, grad_neigh * grad_scale)


def solution(mesh):
    placed = (
        P(("row", "col"), None),
        P(("row", "col"), None),
        P(("row", "col")),
        P(),
        P(),
        P(),
        P("row", "col", None),
        P("row", "col"),
        P("row", "col", None, None, None),
    )
    return jax.shard_map(
        shards,
        mesh=mesh,
        in_specs=placed,
        out_specs=(P(("row", "col"), None), P(("row", "col"), None), P(), P()),
        check_vma=False,
    )
```

profile of v0, /device:TPU:0, one launch (start us, length us, event | category | flops | bytes accessed | tf_op | source)
XLA Modules:
  0.0 546.3 jit_solution(3008152126363309649)
XLA Ops:
  11.3 41.9 %all-gather.2.cloned.1.call-done = bf16[2048,256]{1,0:T(8,128)(2,1)} async-done(((bf16[256,256]{1,0:T(8,128)(2,1)}), bf16[2048,256]{1,0:T(8,128)(2,1)}) %all-gather.2.cloned.1.call-update) | async-done | bytes 1048592 | tf_op jit(solution)/shard_map/all_gather | solution.py:112
  53.2 2.3 pad_maximum_fusion
  55.6 253.4 %while.30 = (s32[]{:T(128)}, f32[1024,256]{1,0:T(8,128)S(1)}, s32[]{:T(128)}, s32[]{:T(128)}, s32[88]{0:T(128)S(1)}, /*index=5*/s32[88,16,128]{2,1,0:T(8,128)}, ...) while((s32[]{:T(128)}, f32[1024,256]{1,0:T(8,128)S(1)}, ...), condition=%wide.region_4.5_spmd.clone, body=%wide.region_2.4_spmd.clone.sunk | while | flops 67902872 | bytes 5061454 | solution.py:68
  57.0 17.3 %while.32 = (s32[]{:T(128)}, bf16[2304,256]{1,0:T(8,128)(2,1)}, s32[8,2]{0,1:T(2,128)S(1)}, bf16[8,128,256]{2,1,0:T(8,128)(2,1)S(1)}, s32[]{:T(128)}) while((s32[]{:T(128)}, bf16[2304,256]{1,0:T(8,128)(2,1)}, s32[8,2]{0,1:T(2,128)S(1)}, bf16[8,128,256]{2,1,0:T(8,128)(2,1)S(1)}, s32[]{:T(128)}) %tuple.84), condition=%wide.while_cond, body=%wide.while_body.sunk | while | flops 2 | bytes 131177 | solution.py:56
  57.6 1.6 bitcast_dynamic-update-slice_fusion.2
  59.8 1.6 bitcast_dynamic-update-slice_fusion.2
  61.9 1.6 bitcast_dynamic-update-slice_fusion.2
  64.1 1.6 bitcast_dynamic-update-slice_fusion.2
  68.4 1.6 bitcast_dynamic-update-slice_fusion.2
  70.6 1.6 bitcast_dynamic-update-slice_fusion.2
  75.0 1.7 gather_fusion.4
  80.0 17.3 %while.32 = (s32[]{:T(128)}, bf16[2304,256]{1,0:T(8,128)(2,1)}, s32[8,2]{0,1:T(2,128)S(1)}, bf16[8,128,256]{2,1,0:T(8,128)(2,1)S(1)}, s32[]{:T(128)}) while((s32[]{:T(128)}, bf16[2304,256]{1,0:T(8,128)(2,1)}, s32[8,2]{0,1:T(2,128)S(1)}, bf16[8,128,256]{2,1,0:T(8,128)(2,1)S(1)}, s32[]{:T(128)}) %tuple.84), condition=%wide.while_cond, body=%wide.while_body.sunk | while | flops 2 | bytes 131177 | solution.py:56
  80.6 1.6 bitcast_dynamic-update-slice_fusion.2
  82.8 1.6 bitcast_dynamic-update-slice_fusion.2
  98.1 1.7 gather_fusion.4
  103.1 17.3 %while.32 = (s32[]{:T(128)}, bf16[2304,256]{1,0:T(8,128)(2,1)}, s32[8,2]{0,1:T(2,128)S(1)}, bf16[8,128,256]{2,1,0:T(8,128)(2,1)S(1)}, s32[]{:T(128)}) while((s32[]{:T(128)}, bf16[2304,256]{1,0:T(8,128)(2,1)}, s32[8,2]{0,1:T(2,128)S(1)}, bf16[8,128,256]{2,1,0:T(8,128)(2,1)S(1)}, s32[]{:T(128)}) %tuple.84), condition=%wide.while_cond, body=%wide.while_body.sunk | while | flops 2 | bytes 131177 | solution.py:56
  121.1 1.7 gather_fusion.4
  126.1 17.3 %while.32 = (s32[]{:T(128)}, bf16[2304,256]{1,0:T(8,128)(2,1)}, s32[8,2]{0,1:T(2,128)S(1)}, bf16[8,128,256]{2,1,0:T(8,128)(2,1)S(1)}, s32[]{:T(128)}) while((s32[]{:T(128)}, bf16[2304,256]{1,0:T(8,128)(2,1)}, s32[8,2]{0,1:T(2,128)S(1)}, bf16[8,128,256]{2,1,0:T(8,128)(2,1)S(1)}, s32[]{:T(128)}) %tuple.84), condition=%wide.while_cond, body=%wide.while_body.sunk | while | flops 2 | bytes 131177 | solution.py:56
  144.2 1.7 gather_fusion.4
  149.2 17.3 %while.32 = (s32[]{:T(128)}, bf16[2304,256]{1,0:T(8,128)(2,1)}, s32[8,2]{0,1:T(2,128)S(1)}, bf16[8,128,256]{2,1,0:T(8,128)(2,1)S(1)}, s32[]{:T(128)}) while((s32[]{:T(128)}, bf16[2304,256]{1,0:T(8,128)(2,1)}, s32[8,2]{0,1:T(2,128)S(1)}, bf16[8,128,256]{2,1,0:T(8,128)(2,1)S(1)}, s32[]{:T(128)}) %tuple.84), condition=%wide.while_cond, body=%wide.while_body.sunk | while | flops 2 | bytes 131177 | solution.py:56
  167.2 1.7 gather_fusion.4
  172.2 17.3 %while.32 = (s32[]{:T(128)}, bf16[2304,256]{1,0:T(8,128)(2,1)}, s32[8,2]{0,1:T(2,128)S(1)}, bf16[8,128,256]{2,1,0:T(8,128)(2,1)S(1)}, s32[]{:T(128)}) while((s32[]{:T(128)}, bf16[2304,256]{1,0:T(8,128)(2,1)}, s32[8,2]{0,1:T(2,128)S(1)}, bf16[8,128,256]{2,1,0:T(8,128)(2,1)S(1)}, s32[]{:T(128)}) %tuple.84), condition=%wide.while_cond, body=%wide.while_body.sunk | while | flops 2 | bytes 131177 | solution.py:56
  190.2 1.7 gather_fusion.4
  195.2 17.3 %while.32 = (s32[]{:T(128)}, bf16[2304,256]{1,0:T(8,128)(2,1)}, s32[8,2]{0,1:T(2,128)S(1)}, bf16[8,128,256]{2,1,0:T(8,128)(2,1)S(1)}, s32[]{:T(128)}) while((s32[]{:T(128)}, bf16[2304,256]{1,0:T(8,128)(2,1)}, s32[8,2]{0,1:T(2,128)S(1)}, bf16[8,128,256]{2,1,0:T(8,128)(2,1)S(1)}, s32[]{:T(128)}) %tuple.84), condition=%wide.while_cond, body=%wide.while_body.sunk | while | flops 2 | bytes 131177 | solution.py:56
  213.3 1.7 gather_fusion.4
  218.3 17.3 %while.32 = (s32[]{:T(128)}, bf16[2304,256]{1,0:T(8,128)(2,1)}, s32[8,2]{0,1:T(2,128)S(1)}, bf16[8,128,256]{2,1,0:T(8,128)(2,1)S(1)}, s32[]{:T(128)}) while((s32[]{:T(128)}, bf16[2304,256]{1,0:T(8,128)(2,1)}, s32[8,2]{0,1:T(2,128)S(1)}, bf16[8,128,256]{2,1,0:T(8,128)(2,1)S(1)}, s32[]{:T(128)}) %tuple.84), condition=%wide.while_cond, body=%wide.while_body.sunk | while | flops 2 | bytes 131177 | solution.py:56
  236.3 1.7 gather_fusion.4
  241.3 17.3 %while.32 = (s32[]{:T(128)}, bf16[2304,256]{1,0:T(8,128)(2,1)}, s32[8,2]{0,1:T(2,128)S(1)}, bf16[8,128,256]{2,1,0:T(8,128)(2,1)S(1)}, s32[]{:T(128)}) while((s32[]{:T(128)}, bf16[2304,256]{1,0:T(8,128)(2,1)}, s32[8,2]{0,1:T(2,128)S(1)}, bf16[8,128,256]{2,1,0:T(8,128)(2,1)S(1)}, s32[]{:T(128)}) %tuple.84), condition=%wide.while_cond, body=%wide.while_body.sunk | while | flops 2 | bytes 131177 | solution.py:56
  259.3 1.7 gather_fusion.4
  264.3 17.3 %while.32 = (s32[]{:T(128)}, bf16[2304,256]{1,0:T(8,128)(2,1)}, s32[8,2]{0,1:T(2,128)S(1)}, bf16[8,128,256]{2,1,0:T(8,128)(2,1)S(1)}, s32[]{:T(128)}) while((s32[]{:T(128)}, bf16[2304,256]{1,0:T(8,128)(2,1)}, s32[8,2]{0,1:T(2,128)S(1)}, bf16[8,128,256]{2,1,0:T(8,128)(2,1)S(1)}, s32[]{:T(128)}) %tuple.84), condition=%wide.while_cond, body=%wide.while_body.sunk | while | flops 2 | bytes 131177 | solution.py:56
  282.4 1.7 gather_fusion.4
  287.4 17.3 %while.32 = (s32[]{:T(128)}, bf16[2304,256]{1,0:T(8,128)(2,1)}, s32[8,2]{0,1:T(2,128)S(1)}, bf16[8,128,256]{2,1,0:T(8,128)(2,1)S(1)}, s32[]{:T(128)}) while((s32[]{:T(128)}, bf16[2304,256]{1,0:T(8,128)(2,1)}, s32[8,2]{0,1:T(2,128)S(1)}, bf16[8,128,256]{2,1,0:T(8,128)(2,1)S(1)}, s32[]{:T(128)}) %tuple.84), condition=%wide.while_cond, body=%wide.while_body.sunk | while | flops 2 | bytes 131177 | solution.py:56
  305.4 1.7 gather_fusion.4
  310.2 20.3 %reduce-scatter.3.cloned.1.call-done = bf16[256,256]{1,0:T(8,128)(2,1)} async-done(((bf16[1024,256]{1,0:T(8,128)(2,1)}), bf16[256,256]{1,0:T(8,128)(2,1)}) %reduce-scatter.3.cloned.1.call-update) | async-done | bytes 131088 | tf_op jit(solution)/shard_map/reduce_scatter | solution.py:114
  330.5 2.0 multiply_convert_fusion
  333.6 6.6 %all_gather.7 = bf16[1024,256]{1,0:T(8,128)(2,1)S(1)} all-gather(bf16[256,256]{1,0:T(8,128)(2,1)S(1)} %fusion.42), channel_id=1, replica_groups=mesh['row'=8,'col'=4] {'col'}, dimensions={0}, use_global_device_ids=true | all-gather | bytes 655360 | tf_op jit(solution)/shard_map/all_gather | solution.py:140
  341.3 1.6 broadcast_in_dim.8
  342.8 87.3 %while.31 = (s32[]{:T(128)}, f32[16,128,256]{2,1,0:T(8,128)}, s32[]{:T(128)}, s32[]{:T(128)}, s32[88]{0:T(128)S(1)}, /*index=5*/s32[88,16,128]{2,1,0:T(8,128)}, ...) while((s32[]{:T(128)}, f32[16,128,256]{2,1,0:T(8,128)}, s32[]{:T(128)}, ...), condition=%wide.region_8.9_spmd.clone, body=%wide.region_6.8_spmd.clone.sunk | while | flops 67897608 | bytes 5974609 | solution.py:101
  345.5 1.7 gather_fusion.2
  347.5 3.3 scatter_fusion
  353.4 1.7 gather_fusion.2
  355.5 3.1 scatter_fusion
  361.2 1.7 gather_fusion.2
  363.2 3.1 scatter_fusion
  369.0 1.7 gather_fusion.2
  371.0 3.3 scatter_fusion
  376.9 1.7 gather_fusion.2
  379.0 3.1 scatter_fusion
  384.7 1.7 gather_fusion.2
  386.7 3.3 scatter_fusion
  392.7 1.7 gather_fusion.2
  394.7 3.4 scatter_fusion
  400.7 1.7 gather_fusion.2
  402.8 3.4 scatter_fusion
  408.8 1.7 gather_fusion.2
  410.8 3.2 scatter_fusion
  416.6 1.7 gather_fusion.2
  418.7 3.3 scatter_fusion
  424.6 1.7 gather_fusion.2
  426.6 3.5 scatter_fusion
  430.1 2.7 convert_element_type.88
  432.8 38.5 %all-reduce.4.cloned.1.call-done = (f32[256,256]{0,1:T(8,128)}, f32[256,256]{0,1:T(8,128)}) async-done(((f32[256,256]{0,1:T(8,128)}, f32[256,256]{0,1:T(8,128)}), (f32[256,256]{0,1:T(8,128)}, f32[256,256]{0,1:T(8,128)})) %all-reduce.4.cloned.1.call-update) | async-done | bytes 524304 | tf_op jit(solution)/shard_map/psum | solution.py:134
  474.1 63.9 %reduce-scatter.5.cloned.1.call-done = bf16[256,256]{1,0:T(8,128)(2,1)} async-done(((bf16[2048,256]{1,0:T(8,128)(2,1)}), bf16[256,256]{1,0:T(8,128)(2,1)}) %reduce-scatter.5.cloned.1.call-update) | async-done | bytes 131088 | tf_op jit(solution)/shard_map/reduce_scatter | solution.py:142
  538.0 1.8 fusion.41
  (545 shorter events, 245.6 us)
Async XLA Ops:
  7.2 323.3 %copy-start = (bf16[256,256]{1,0:T(8,128)(2,1)S(1)}, bf16[256,256]{1,0:T(8,128)(2,1)}, u32[]{:S(2)}) copy-start(bf16[256,256]{1,0:T(8,128)(2,1)} %param.17) | copy-start | bytes 393220
  7.2 48.4 %copy-start.1 = (s32[1,1,88]{2,1,0:T(1,128)S(1)}, s32[1,1,88]{2,1,0:T(1,128)}, u32[]{:S(2)}) copy-start(s32[1,1,88]{2,1,0:T(1,128)} %param.19) | copy-start | bytes 1060
  7.2 46.0 %all-gather.2.cloned.1.call-start = ((), (), s32[]{:S(2)}) async-start(), calls=%async_computation.2 | async-start | bytes 1179648 | tf_op jit(solution)/shard_map/all_gather | solution.py:112
  7.9 322.6 %reduce-scatter.3.cloned.1.call-start = ((), (), s32[]{:S(2)}) async-start(), calls=%async_computation.3 | async-start | bytes 655360 | tf_op jit(solution)/shard_map/reduce_scatter | solution.py:114
  309.0 1.0 copy-start.4
  309.0 1.0 copy-start.2
  309.0 1.0 copy-start.3
  309.0 21.5 %copy-start.5 = (bf16[256,256]{1,0:T(8,128)(2,1)S(1)}, bf16[256,256]{1,0:T(8,128)(2,1)}, u32[]{:S(2)}) copy-start(bf16[256,256]{1,0:T(8,128)(2,1)} %param.14) | copy-start | bytes 393220
  309.0 21.4 %copy-start.7 = (f32[256]{0:T(256)S(1)}, f32[256]{0:T(256)}, u32[]{:S(2)}) copy-start(f32[256]{0:T(256)} %param.18) | copy-start | bytes 3076
  309.9 161.4 %all-reduce.4.cloned.1.call-start = ((), (), s32[]{:S(2)}) async-start(), calls=%async_computation.5 | async-start | bytes 1048576 | tf_op jit(solution)/shard_map/psum | solution.py:134
  330.5 9.7 %copy-start.6 = (bf16[256,256]{1,0:T(8,128)(2,1)S(1)}, bf16[256,256]{1,0:T(8,128)(2,1)}, u32[]{:S(2)}) copy-start(bf16[256,256]{1,0:T(8,128)(2,1)} %reduce-scatter.3.cloned.1.call-done) | copy-start | bytes 393220
  341.2 196.7 %reduce-scatter.5.cloned.1.call-start = ((), (), s32[]{:S(2)}) async-start(), calls=%async_computation.4 | async-start | bytes 1179648 | tf_op jit(solution)/shard_map/reduce_scatter | solution.py:142
Sparse Core Ops, SparseCore 0:
  10.1 42.9 all-gather.1
  310.1 20.3 reduce-scatter.2
  341.3 129.9 all-reduce.3
  474.6 63.3 reduce-scatter.4
where the time goes:
time: 553 us; the launch traced here: 546 us
  local copies, waits for them, and re-layouts  251 us (45%)
  waiting for transfers between devices  165 us (30%)
  other arithmetic  72.9 us (13%)
  loops' own time  18.5 us (3%)
  matrix products  16.1 us (3%)
  between operations  15.8 us (3%)
  blocking collectives  6.59 us (1%)
    gather x264, local copies, waits for them, and re-layouts  188 us
    reduce_scatter x1, waiting for transfers between devices, shards(): lax.psum_scatter(spread_rows(0, panel_size, slot_ids, live_count, mask_wo...  63.9 us
    all_gather x1, waiting for transfers between devices, shards(): panel = lax.all_gather(features, 'row', axis=0, tiled=True)  41.9 us
    psum x1, waiting for transfers between devices, shards(): grad_self, grad_neigh = lax.psum((grad_self, grad_neigh), ('row', 'col'))  38.5 us
    scatter-add x11, other arithmetic, spread_one_group(): return running.at[column_block - first_block].add(products)  35.9 us
    reduce_scatter x1, waiting for transfers between devices, shards(): lax.psum_scatter(partial_value.astype(jnp.bfloat16), 'col', scatter_dimen...  20.3 us
    gather x11, local copies, waits for them, and re-layouts, spread_one_group(): mask_words[chosen]  18.3 us
    gather x11, local copies, waits for them, and re-layouts, aggregate_one_group(): mask_words[chosen]  18.3 us
  transfers between devices with their start and end apart: 4, of which 4 were waited for; matrix products, arithmetic and copies ran while one was open for 16% of the time, Pallas kernels for 0%

commit v1 on v0

--- a/solution.py
+++ b/solution.py
@@ -5,6 +5,19 @@
 from jax.sharding import PartitionSpec as P
 
 group_tiles = 8
+
+
+def ring_gather(x, axis, dim):
+    ways = lax.axis_size(axis)
+    up = [(d, (d + 1) % ways) for d in range(ways)]
+    down = [(d, (d - 1) % ways) for d in range(ways)]
+    earlier, later = ([x], [x])
+    for _ in range(ways // 2):
+        earlier.append(lax.ppermute(earlier[-1], axis, up))
+    for _ in range((ways - 1) // 2):
+        later.append(lax.ppermute(later[-1], axis, down))
+    line = jnp.concatenate([*earlier[::-1], *later[1:]], axis=dim)
+    return jnp.roll(line, (lax.axis_index(axis) - ways // 2) * x.shape[dim], axis=dim)
 
 
 def unpack_tiles(mask_words):
@@ -109,7 +122,7 @@
     node_rows, feature_width = features.shape
     group_size = node_rows * lax.axis_size("col")
     initial = jnp.zeros((group_size, feature_width), jnp.float32)
-    panel = lax.all_gather(features, "row", axis=0, tiled=True)
+    panel = ring_gather(features, "row", 0)
     partial_value = aggregate_piece(initial, panel, 0, slot_ids, live_count, mask_words)
     summed = lax.psum_scatter(
         partial_value.astype(jnp.bfloat16), "col", scatter_dimension=0, tiled=True

time: 553 us -> 545 us (0.986)
  waiting for transfers between devices: 165 us -> 141 us
  starting transfers between devices: 0.16 us -> 17.4 us
    all_gather x1 -> x0, waiting for transfers between devices: 41.9 us -> none  [shards(): panel = lax.all_gather(features, 'row', axis=0, tiled=True)]
    ppermute x0 -> x7, starting transfers between devices: none -> 17.3 us  [the longest x3 14.2 us: ring_gather(): later.append(lax.ppermute(later[-1], axis, down))]
    ppermute x0 -> x7, waiting for transfers between devices: none -> 14.1 us  [the longest x4 12.4 us: ring_gather(): earlier.append(lax.ppermute(earlier[-1], axis, up))]
  transfers between devices with their start and end apart: 4 -> 10, of which waited for: 4 -> 8; matrix products, arithmetic and copies ran while one was open for 16% -> 16% of each run, Pallas kernels for 0% -> 0%
where the time goes in v1:
time: 545 us; the launch traced here: 538 us
  local copies, waits for them, and re-layouts  252 us (46%)
  waiting for transfers between devices  141 us (26%)
  other arithmetic  72 us (13%)
  starting transfers between devices  17.4 us (3%)
  loops' own time  17.3 us (3%)
  matrix products  16.1 us (3%)
  between operations  16 us (3%)
  blocking collectives  6.59 us (1%)
    gather x264, local copies, waits for them, and re-layouts  188 us
    reduce_scatter x1, waiting for transfers between devices, shards(): lax.psum_scatter(spread_rows(0, panel_size, slot_ids, live_count, mask_wo...  64 us
    psum x1, waiting for transfers between devices, shards(): grad_self, grad_neigh = lax.psum((grad_self, grad_neigh), ('row', 'col'))  39.2 us
    scatter-add x11, other arithmetic, spread_one_group(): return running.at[column_block - first_block].add(products)  35.2 us
    reduce_scatter x1, waiting for transfers between devices, shards(): lax.psum_scatter(partial_value.astype(jnp.bfloat16), 'col', scatter_dimen...  23.3 us
    gather x11, local copies, waits for them, and re-layouts, spread_one_group(): mask_words[chosen]  18.3 us
    gather x11, local copies, waits for them, and re-layouts, aggregate_one_group(): mask_words[chosen]  18.3 us
    scatter-add x11, other arithmetic, aggregate_one_group(): return shaped.at[row_block].add(products).reshape(running.shape)  14.7 us
  transfers between devices with their start and end apart: 10, of which 8 were waited for; matrix products, arithmetic and copies ran while one was open for 16% of the time, Pallas kernels for 0%

profile of v1, /device:TPU:0, one launch (start us, length us, event | category | flops | bytes accessed | tf_op | source)
XLA Modules:
  0.0 538.2 jit_solution(14736770928936795774)
XLA Ops:
  7.2 3.0 collective-permute-start
  10.3 6.7 %collective-permute-done = bf16[256,256]{1,0:T(8,128)(2,1)S(1)} collective-permute-done((bf16[256,256]{1,0:T(8,128)(2,1)}, bf16[256,256]{1,0:T(8,128)(2,1)S(1)}, u32[]{:S(2)}, u32[]{:S(2)}) %collective-permute-start) | collective-permute-done | bytes 131104 | tf_op jit(solution)/shard_map/ppermute | solution.py:16
  17.0 4.7 collective-permute-start.4
  21.7 2.9 collective-permute-done.1
  25.0 4.7 collective-permute-start.5
  29.7 2.7 collective-permute-done.2
  35.7 4.8 collective-permute-start.6
  44.4 253.3 %while.30 = (s32[]{:T(128)}, f32[1024,256]{1,0:T(8,128)S(1)}, s32[]{:T(128)}, s32[]{:T(128)}, s32[88]{0:T(128)S(1)}, /*index=5*/s32[88,16,128]{2,1,0:T(8,128)}, ...) while((s32[]{:T(128)}, f32[1024,256]{1,0:T(8,128)S(1)}, ...), condition=%wide.region_4.5_spmd.clone, body=%wide.region_2.4_spmd.clone.sunk | while | flops 67902872 | bytes 5061454 | solution.py:81
  45.8 17.3 %while.32 = (s32[]{:T(128)}, bf16[2304,256]{1,0:T(8,128)(2,1)}, s32[8,2]{0,1:T(2,128)S(1)}, bf16[8,128,256]{2,1,0:T(8,128)(2,1)S(1)}, s32[]{:T(128)}) while((s32[]{:T(128)}, bf16[2304,256]{1,0:T(8,128)(2,1)}, s32[8,2]{0,1:T(2,128)S(1)}, bf16[8,128,256]{2,1,0:T(8,128)(2,1)S(1)}, s32[]{:T(128)}) %tuple.84), condition=%wide.while_cond, body=%wide.while_body.sunk | while | flops 2 | bytes 131177 | solution.py:69
  46.4 1.6 bitcast_dynamic-update-slice_fusion.2
  48.6 1.6 bitcast_dynamic-update-slice_fusion.2
  50.7 1.6 bitcast_dynamic-update-slice_fusion.2
  52.9 1.6 bitcast_dynamic-update-slice_fusion.2
  63.9 1.7 gather_fusion.4
  68.8 17.3 %while.32 = (s32[]{:T(128)}, bf16[2304,256]{1,0:T(8,128)(2,1)}, s32[8,2]{0,1:T(2,128)S(1)}, bf16[8,128,256]{2,1,0:T(8,128)(2,1)S(1)}, s32[]{:T(128)}) while((s32[]{:T(128)}, bf16[2304,256]{1,0:T(8,128)(2,1)}, s32[8,2]{0,1:T(2,128)S(1)}, bf16[8,128,256]{2,1,0:T(8,128)(2,1)S(1)}, s32[]{:T(128)}) %tuple.84), condition=%wide.while_cond, body=%wide.while_body.sunk | while | flops 2 | bytes 131177 | solution.py:69
  86.9 1.7 gather_fusion.4
  91.9 17.3 %while.32 = (s32[]{:T(128)}, bf16[2304,256]{1,0:T(8,128)(2,1)}, s32[8,2]{0,1:T(2,128)S(1)}, bf16[8,128,256]{2,1,0:T(8,128)(2,1)S(1)}, s32[]{:T(128)}) while((s32[]{:T(128)}, bf16[2304,256]{1,0:T(8,128)(2,1)}, s32[8,2]{0,1:T(2,128)S(1)}, bf16[8,128,256]{2,1,0:T(8,128)(2,1)S(1)}, s32[]{:T(128)}) %tuple.84), condition=%wide.while_cond, body=%wide.while_body.sunk | while | flops 2 | bytes 131177 | solution.py:69
  110.0 1.7 gather_fusion.4
  114.9 17.3 %while.32 = (s32[]{:T(128)}, bf16[2304,256]{1,0:T(8,128)(2,1)}, s32[8,2]{0,1:T(2,128)S(1)}, bf16[8,128,256]{2,1,0:T(8,128)(2,1)S(1)}, s32[]{:T(128)}) while((s32[]{:T(128)}, bf16[2304,256]{1,0:T(8,128)(2,1)}, s32[8,2]{0,1:T(2,128)S(1)}, bf16[8,128,256]{2,1,0:T(8,128)(2,1)S(1)}, s32[]{:T(128)}) %tuple.84), condition=%wide.while_cond, body=%wide.while_body.sunk | while | flops 2 | bytes 131177 | solution.py:69
  133.0 1.7 gather_fusion.4
  137.9 17.3 %while.32 = (s32[]{:T(128)}, bf16[2304,256]{1,0:T(8,128)(2,1)}, s32[8,2]{0,1:T(2,128)S(1)}, bf16[8,128,256]{2,1,0:T(8,128)(2,1)S(1)}, s32[]{:T(128)}) while((s32[]{:T(128)}, bf16[2304,256]{1,0:T(8,128)(2,1)}, s32[8,2]{0,1:T(2,128)S(1)}, bf16[8,128,256]{2,1,0:T(8,128)(2,1)S(1)}, s32[]{:T(128)}) %tuple.84), condition=%wide.while_cond, body=%wide.while_body.sunk | while | flops 2 | bytes 131177 | solution.py:69
  156.0 1.7 gather_fusion.4
  161.0 17.3 %while.32 = (s32[]{:T(128)}, bf16[2304,256]{1,0:T(8,128)(2,1)}, s32[8,2]{0,1:T(2,128)S(1)}, bf16[8,128,256]{2,1,0:T(8,128)(2,1)S(1)}, s32[]{:T(128)}) while((s32[]{:T(128)}, bf16[2304,256]{1,0:T(8,128)(2,1)}, s32[8,2]{0,1:T(2,128)S(1)}, bf16[8,128,256]{2,1,0:T(8,128)(2,1)S(1)}, s32[]{:T(128)}) %tuple.84), condition=%wide.while_cond, body=%wide.while_body.sunk | while | flops 2 | bytes 131177 | solution.py:69
  179.1 1.7 gather_fusion.4
  184.0 17.3 %while.32 = (s32[]{:T(128)}, bf16[2304,256]{1,0:T(8,128)(2,1)}, s32[8,2]{0,1:T(2,128)S(1)}, bf16[8,128,256]{2,1,0:T(8,128)(2,1)S(1)}, s32[]{:T(128)}) while((s32[]{:T(128)}, bf16[2304,256]{1,0:T(8,128)(2,1)}, s32[8,2]{0,1:T(2,128)S(1)}, bf16[8,128,256]{2,1,0:T(8,128)(2,1)S(1)}, s32[]{:T(128)}) %tuple.84), condition=%wide.while_cond, body=%wide.while_body.sunk | while | flops 2 | bytes 131177 | solution.py:69
  202.1 1.7 gather_fusion.4
  207.0 17.3 %while.32 = (s32[]{:T(128)}, bf16[2304,256]{1,0:T(8,128)(2,1)}, s32[8,2]{0,1:T(2,128)S(1)}, bf16[8,128,256]{2,1,0:T(8,128)(2,1)S(1)}, s32[]{:T(128)}) while((s32[]{:T(128)}, bf16[2304,256]{1,0:T(8,128)(2,1)}, s32[8,2]{0,1:T(2,128)S(1)}, bf16[8,128,256]{2,1,0:T(8,128)(2,1)S(1)}, s32[]{:T(128)}) %tuple.84), condition=%wide.while_cond, body=%wide.while_body.sunk | while | flops 2 | bytes 131177 | solution.py:69
  225.1 1.7 gather_fusion.4
  230.0 17.3 %while.32 = (s32[]{:T(128)}, bf16[2304,256]{1,0:T(8,128)(2,1)}, s32[8,2]{0,1:T(2,128)S(1)}, bf16[8,128,256]{2,1,0:T(8,128)(2,1)S(1)}, s32[]{:T(128)}) while((s32[]{:T(128)}, bf16[2304,256]{1,0:T(8,128)(2,1)}, s32[8,2]{0,1:T(2,128)S(1)}, bf16[8,128,256]{2,1,0:T(8,128)(2,1)S(1)}, s32[]{:T(128)}) %tuple.84), condition=%wide.while_cond, body=%wide.while_body.sunk | while | flops 2 | bytes 131177 | solution.py:69
  248.1 1.7 gather_fusion.4
  253.1 17.3 %while.32 = (s32[]{:T(128)}, bf16[2304,256]{1,0:T(8,128)(2,1)}, s32[8,2]{0,1:T(2,128)S(1)}, bf16[8,128,256]{2,1,0:T(8,128)(2,1)S(1)}, s32[]{:T(128)}) while((s32[]{:T(128)}, bf16[2304,256]{1,0:T(8,128)(2,1)}, s32[8,2]{0,1:T(2,128)S(1)}, bf16[8,128,256]{2,1,0:T(8,128)(2,1)S(1)}, s32[]{:T(128)}) %tuple.84), condition=%wide.while_cond, body=%wide.while_body.sunk | while | flops 2 | bytes 131177 | solution.py:69
  271.2 1.7 gather_fusion.4
  276.1 17.3 %while.32 = (s32[]{:T(128)}, bf16[2304,256]{1,0:T(8,128)(2,1)}, s32[8,2]{0,1:T(2,128)S(1)}, bf16[8,128,256]{2,1,0:T(8,128)(2,1)S(1)}, s32[]{:T(128)}) while((s32[]{:T(128)}, bf16[2304,256]{1,0:T(8,128)(2,1)}, s32[8,2]{0,1:T(2,128)S(1)}, bf16[8,128,256]{2,1,0:T(8,128)(2,1)S(1)}, s32[]{:T(128)}) %tuple.84), condition=%wide.while_cond, body=%wide.while_body.sunk | while | flops 2 | bytes 131177 | solution.py:69
  294.2 1.7 gather_fusion.4
  299.0 23.3 %reduce-scatter.3.cloned.1.call-done = bf16[256,256]{1,0:T(8,128)(2,1)} async-done(((bf16[1024,256]{1,0:T(8,128)(2,1)}), bf16[256,256]{1,0:T(8,128)(2,1)}) %reduce-scatter.3.cloned.1.call-update) | async-done | bytes 131088 | tf_op jit(solution)/shard_map/reduce_scatter | solution.py:127
  322.3 2.0 multiply_convert_fusion
  325.4 6.6 %all_gather.3 = bf16[1024,256]{1,0:T(8,128)(2,1)S(1)} all-gather(bf16[256,256]{1,0:T(8,128)(2,1)S(1)} %fusion.42), channel_id=1, replica_groups=mesh['row'=8,'col'=4] {'col'}, dimensions={0}, use_global_device_ids=true | all-gather | bytes 655360 | tf_op jit(solution)/shard_map/all_gather | solution.py:153
  334.6 86.6 %while.31 = (s32[]{:T(128)}, f32[16,128,256]{2,1,0:T(8,128)}, s32[]{:T(128)}, s32[]{:T(128)}, s32[88]{0:T(128)S(1)}, /*index=5*/s32[88,16,128]{2,1,0:T(8,128)}, ...) while((s32[]{:T(128)}, f32[16,128,256]{2,1,0:T(8,128)}, s32[]{:T(128)}, ...), condition=%wide.region_8.9_spmd.clone, body=%wide.region_6.8_spmd.clone.sunk | while | flops 67897608 | bytes 5974609 | solution.py:114
  337.3 1.7 gather_fusion.2
  339.3 3.3 scatter_fusion
  345.2 1.7 gather_fusion.2
  347.3 3.2 scatter_fusion
  353.1 1.7 gather_fusion.2
  355.1 3.1 scatter_fusion
  360.9 1.7 gather_fusion.2
  362.9 3.2 scatter_fusion
  368.8 1.7 gather_fusion.2
  370.8 3.1 scatter_fusion
  376.6 1.7 gather_fusion.2
  378.6 3.1 scatter_fusion
  384.4 1.7 gather_fusion.2
  386.4 3.2 scatter_fusion
  392.3 1.7 gather_fusion.2
  394.3 3.4 scatter_fusion
  400.4 1.7 gather_fusion.2
  402.4 3.1 scatter_fusion
  408.2 1.7 gather_fusion.2
  410.2 3.1 scatter_fusion
  416.0 1.7 gather_fusion.2
  418.0 3.2 scatter_fusion
  421.2 2.7 convert_element_type.88
  423.9 39.2 %all-reduce.4.cloned.1.call-done = (f32[256,256]{0,1:T(8,128)}, f32[256,256]{0,1:T(8,128)}) async-done(((f32[256,256]{0,1:T(8,128)}, f32[256,256]{0,1:T(8,128)}), (f32[256,256]{0,1:T(8,128)}, f32[256,256]{0,1:T(8,128)})) %all-reduce.4.cloned.1.call-update) | async-done | bytes 524304 | tf_op jit(solution)/shard_map/psum | solution.py:147
  465.9 64.0 %reduce-scatter.5.cloned.1.call-done = bf16[256,256]{1,0:T(8,128)(2,1)} async-done(((bf16[2048,256]{1,0:T(8,128)(2,1)}), bf16[256,256]{1,0:T(8,128)(2,1)}) %reduce-scatter.5.cloned.1.call-update) | async-done | bytes 131088 | tf_op jit(solution)/shard_map/reduce_scatter | solution.py:155
  529.9 1.8 fusion.41
  (573 shorter events, 257.7 us)
Async XLA Ops:
  7.2 315.1 %copy-start = (bf16[256,256]{1,0:T(8,128)(2,1)S(1)}, bf16[256,256]{1,0:T(8,128)(2,1)}, u32[]{:S(2)}) copy-start(bf16[256,256]{1,0:T(8,128)(2,1)} %param.17) | copy-start | bytes 393220
  7.2 35.9 %copy-start.2 = (bf16[256,256]{1,0:T(8,128)(2,1)S(1)}, bf16[256,256]{1,0:T(8,128)(2,1)}, u32[]{:S(2)}) copy-start(bf16[256,256]{1,0:T(8,128)(2,1)} %param.13) | copy-start | bytes 393220
  7.2 315.1 %reduce-scatter.3.cloned.1.call-start = ((), (), s32[]{:S(2)}) async-start(), calls=%async_computation.2 | async-start | bytes 655360 | tf_op jit(solution)/shard_map/reduce_scatter | solution.py:127
  7.2 9.8 %collective-permute-start = (bf16[256,256]{1,0:T(8,128)(2,1)}, bf16[256,256]{1,0:T(8,128)(2,1)S(1)}, u32[]{:S(2)}, u32[]{:S(2)}) collective-permute-start(bf16[256,256]{1,0:T(8,128)(2,1)} %param.13), channel_id=1, source_target_pairs={{0,4},{4,8},{8,12},{12,16},{16,20},{20,24},{24,28},{28,0},{1,5},{5... | collective-permute-start | bytes 393224 | tf_op jit(solution)/shard_map/ppermute | solution.py:16
  17.0 7.7 %collective-permute-start.1 = (bf16[256,256]{1,0:T(8,128)(2,1)S(1)}, bf16[256,256]{1,0:T(8,128)(2,1)S(1)}, u32[]{:S(2)}, u32[]{:S(2)}) collective-permute-start(bf16[256,256]{1,0:T(8,128)(2,1)S(1)} %collective-permute-done), channel_id=1, source_target_pairs={{0,4},{4,8},{8,12},{12,16},{16,20},{20,24},{24,28},{28,0},{1,5},{5... | collective-permute-start | bytes 393224 | tf_op jit(solution)/shard_map/ppermute | solution.py:16
  17.0 8.0 %collective-permute-start.4 = (bf16[256,256]{1,0:T(8,128)(2,1)}, bf16[256,256]{1,0:T(8,128)(2,1)S(1)}, u32[]{:S(2)}, u32[]{:S(2)}) collective-permute-start(bf16[256,256]{1,0:T(8,128)(2,1)} %param.13), channel_id=1, source_target_pairs={{0,28},{4,0},{8,4},{12,8},{16,12},{20,16},{24,20},{28,24},{1,29},{... | collective-permute-start | bytes 393224 | tf_op jit(solution)/shard_map/ppermute | solution.py:18
  24.7 7.7 %collective-permute-start.2 = (bf16[256,256]{1,0:T(8,128)(2,1)S(1)}, bf16[256,256]{1,0:T(8,128)(2,1)S(1)}, u32[]{:S(2)}, u32[]{:S(2)}) collective-permute-start(bf16[256,256]{1,0:T(8,128)(2,1)S(1)} %collective-permute-done.1), channel_id=1, source_target_pairs={{0,4},{4,8},{8,12},{12,16},{16,20},{20,24},{24,28},{28,0},{1,5},{5... | collective-permute-start | bytes 393224 | tf_op jit(solution)/shard_map/ppermute | solution.py:16
  25.0 10.7 %collective-permute-start.5 = (bf16[256,256]{1,0:T(8,128)(2,1)S(1)}, bf16[256,256]{1,0:T(8,128)(2,1)S(1)}, u32[]{:S(2)}, u32[]{:S(2)}) collective-permute-start(bf16[256,256]{1,0:T(8,128)(2,1)S(1)} %collective-permute-done.4), channel_id=1, source_target_pairs={{0,28},{4,0},{8,4},{12,8},{16,12},{20,16},{24,20},{28,24},{1,29},{... | collective-permute-start | bytes 393224 | tf_op jit(solution)/shard_map/ppermute | solution.py:18
  32.4 8.1 %collective-permute-start.3 = (bf16[256,256]{1,0:T(8,128)(2,1)S(1)}, bf16[256,256]{1,0:T(8,128)(2,1)S(1)}, u32[]{:S(2)}, u32[]{:S(2)}) collective-permute-start(bf16[256,256]{1,0:T(8,128)(2,1)S(1)} %collective-permute-done.2), channel_id=1, source_target_pairs={{0,4},{4,8},{8,12},{12,16},{16,20},{20,24},{24,28},{28,0},{1,5},{5... | collective-permute-start | bytes 393224 | tf_op jit(solution)/shard_map/ppermute | solution.py:16
  35.7 7.3 %collective-permute-start.6 = (bf16[256,256]{1,0:T(8,128)(2,1)S(1)}, bf16[256,256]{1,0:T(8,128)(2,1)S(1)}, u32[]{:S(2)}, u32[]{:S(2)}) collective-permute-start(bf16[256,256]{1,0:T(8,128)(2,1)S(1)} %collective-permute-done.5), channel_id=1, source_target_pairs={{0,28},{4,0},{8,4},{12,8},{16,12},{20,16},{24,20},{28,24},{1,29},{... | collective-permute-start | bytes 393224 | tf_op jit(solution)/shard_map/ppermute | solution.py:18
  43.2 1.2 copy-start.1
  297.8 1.0 copy-start.4
  297.8 1.0 copy-start.3
  297.8 24.5 %copy-start.5 = (bf16[256,256]{1,0:T(8,128)(2,1)S(1)}, bf16[256,256]{1,0:T(8,128)(2,1)}, u32[]{:S(2)}) copy-start(bf16[256,256]{1,0:T(8,128)(2,1)} %param.14) | copy-start | bytes 393220
  297.8 24.5 %copy-start.7 = (f32[256]{0:T(256)S(1)}, f32[256]{0:T(256)}, u32[]{:S(2)}) copy-start(f32[256]{0:T(256)} %param.18) | copy-start | bytes 3076
  298.7 164.5 %all-reduce.4.cloned.1.call-start = ((), (), s32[]{:S(2)}) async-start(), calls=%async_computation.4 | async-start | bytes 1048576 | tf_op jit(solution)/shard_map/psum | solution.py:147
  322.3 9.7 %copy-start.6 = (bf16[256,256]{1,0:T(8,128)(2,1)S(1)}, bf16[256,256]{1,0:T(8,128)(2,1)}, u32[]{:S(2)}) copy-start(bf16[256,256]{1,0:T(8,128)(2,1)} %reduce-scatter.3.cloned.1.call-done) | copy-start | bytes 393220
  333.1 196.8 %reduce-scatter.5.cloned.1.call-start = ((), (), s32[]{:S(2)}) async-start(), calls=%async_computation.3 | async-start | bytes 1179648 | tf_op jit(solution)/shard_map/reduce_scatter | solution.py:155
Sparse Core Ops, SparseCore 0:
  298.8 23.4 reduce-scatter.2
  333.2 129.9 all-reduce.3
  466.6 63.2 reduce-scatter.4
